TPU v7x, 128 devices: a whole 4x4x4 slice. The times are simulated.
128 devices in a mesh: seq: 8 (over y, x_hi), rep: 16 (over x_lo, z, core).
Axes of the slice: x: 4 (x_hi: 2, x_lo: 2; x = x_hi * 2 + x_lo), y: 4, z: 4, core: 2. Of those that a mesh axis runs over, the one named last changes fastest.
Arguments:
- tile_embed: bfloat16 [16, 8192, 768], P('rep', 'seq'), may hold values from -6 to 6
- tile_source: int32 [16, 8192], P('rep', 'seq'), may hold values from 0 to 8191, as said below
- slide_len: int32 [16], P('rep'), may hold values from 4096 to 8192
- grad_out: bfloat16 [16, 8192, 768], P('rep', 'seq'), may hold values from -6 to 6
- w_query: bfloat16 [768, 768], replicated, may hold values from -0.11727427342914273 to 0.11727427342914273
- w_key: bfloat16 [768, 768], replicated, may hold values from -0.11727427342914273 to 0.11727427342914273
- w_value: bfloat16 [768, 768], replicated, may hold values from -0.21875 to 0.21875
- w_out: bfloat16 [768, 768], replicated, may hold values from -0.21875 to 0.21875
Outputs:
- encoded: bfloat16 [16, 8192, 768], P('rep', 'seq')
- embed_grad: bfloat16 [16, 8192, 768], P('rep', 'seq')
- grad_query: float32 [768, 768], replicated
- grad_key: float32 [768, 768], replicated
- grad_value: float32 [768, 768], replicated
- grad_outproj: float32 [768, 768], replicated
Inputs may be any that keep to these rules, and one draw needn't show every extreme that they name: For each slide, tile_source is a permutation of 0 to 8191; each run of 1024 slide positions (aligned) takes exactly 1024 // (number of such runs) rows from each aligned run of 1024 rows of tile_embed.
All inputs are finite; a program needn't handle non-finite values.
Results may differ from a plain program's by a relative error of at most 0.0025.
The roundings to bfloat16 on the way count: a program that leaves them out, or rounds other values in their place, can miss the bound.
Values may be sent and summed in bfloat16 or wider, within the bound.
A program may use at most 192 MiB of HBM per device.

v0:
```python
import jax
import jax.numpy as jnp
from jax import lax
from jax.sharding import PartitionSpec as P

HEADS = 16
SEG = 1024
RATE = 16
NEGATIVE = -1e30


def sent_together(arrays, axis, dim, along):
    both = jnp.concatenate(arrays, axis=along)
    result, at, done = (lax.all_gather(both, axis, axis=dim, tiled=True), 0, [])
    for a in arrays:
        done.append(lax.slice_in_dim(result, at, at + a.shape[along], axis=along))
        at += a.shape[along]
    return tuple(done)


def side_by_side(arrays, axis, dim, along):
    widths = [a.shape[along] for a in arrays]
    both = jnp.concatenate(arrays, axis=along)
    result = lax.psum_scatter(both, axis, scatter_dimension=dim, tiled=True)
    return tuple(jnp.split(result, [sum(widths[:k]) for k in range(1, len(widths))], axis=along))


def chosen(dilation, head_count):
    return jnp.arange(dilation)[:, None] == (jnp.arange(head_count) % dilation)[None, :]


def sparse_rows(dense, dilation):
    row_count, head_count, trailing = dense.shape
    blocks = dense.astype(jnp.float32).reshape(
        row_count // dilation, dilation, head_count, trailing
    )
    selected = chosen(dilation, head_count)[None, :, :, None]
    return jnp.sum(jnp.where(selected, blocks, jnp.float32(0.0)), axis=1)


def spread_rows(sparse, dilation, filler):
    row_count, head_count, trailing = sparse.shape
    selected = chosen(dilation, head_count)[None, :, :, None]
    spread = jnp.where(selected, sparse[:, None], jnp.float32(filler))
    return spread.reshape(row_count * dilation, head_count, trailing)


def product(pattern, left_side, right_side):
    return jnp.einsum(pattern, left_side, right_side, preferred_element_type=jnp.float32)


def masked_scores(queries, key_rows, key_ok, pieces, scaling):
    scores = product("nqd,nkd->nqk", queries, key_rows) * scaling
    return jnp.where(key_ok.reshape(pieces, 1, -1), scores, NEGATIVE)


def head_forward(queries, key_rows, values, key_ok, pieces, scaling):
    head_width = queries.shape[-1]
    queries = queries.reshape(pieces, -1, head_width)
    key_rows = key_rows.reshape(pieces, -1, head_width)
    values = values.reshape(pieces, -1, head_width)
    scores = masked_scores(queries, key_rows, key_ok, pieces, scaling)
    maxima = jnp.max(scores, axis=-1)
    weights = jnp.exp(scores - maxima[..., None])
    totals = jnp.sum(weights, axis=-1)
    numerator = product("nqk,nkd->nqd", weights.astype(jnp.bfloat16), values)
    return (numerator.reshape(-1, head_width), maxima.reshape(-1), totals.reshape(-1))


def split_pieces(arrays, pieces):
    return tuple((member.reshape(pieces, -1, member.shape[-1]) for member in arrays))


def score_terms(queries, key_rows, values, key_ok, log_total, upstream, deltas, pieces, scaling):
    scores = masked_scores(queries, key_rows, key_ok, pieces, scaling)
    probabilities = jnp.exp(scores - log_total.reshape(pieces, -1, 1))
    prob_grad = product("nqd,nkd->nqk", upstream, values)
    score_grad = (probabilities * (prob_grad - deltas.reshape(pieces, -1, 1))).astype(jnp.bfloat16)
    return (probabilities, score_grad)


def head_backward(queries, key_rows, values, key_ok, log_total, upstream, deltas, pieces, scaling):
    head_width = queries.shape[-1]
    queries, key_rows, values, upstream = split_pieces(
        (queries, key_rows, values, upstream), pieces
    )
    probabilities, score_grad = score_terms(
        queries, key_rows, values, key_ok, log_total, upstream, deltas, pieces, scaling
    )
    value_grad = product("nqk,nqd->nkd", probabilities.astype(jnp.bfloat16), upstream)
    query_grad = product("nqk,nkd->nqd", score_grad, key_rows) * scaling
    key_grad = product("nqk,nqd->nkd", score_grad, queries) * scaling
    return (
        query_grad.reshape(-1, head_width),
        key_grad.reshape(-1, head_width),
        value_grad.reshape(-1, head_width),
    )


def heads_map(function, arrays, pieces, scaling):
    transposed = tuple((jnp.moveaxis(member, 1, 0) for member in arrays))
    results = lax.map(lambda members: function(*members, pieces, scaling), transposed)
    return tuple((jnp.moveaxis(member, 0, 1) for member in results))


def merge_parts(local_part, remote, dilation):
    numer_local, max_local, total_local = local_part
    numer_far = spread_rows(remote[0], dilation, 0.0)
    max_far = spread_rows(remote[1][..., None], dilation, NEGATIVE)[..., 0]
    total_far = spread_rows(remote[2][..., None], dilation, 0.0)[..., 0]
    highest = jnp.maximum(max_local, max_far)
    weight_local = jnp.exp(max_local - highest)
    weight_far = jnp.exp(max_far - highest)
    combined = total_local * weight_local + total_far * weight_far
    output = (numer_local * weight_local[..., None] + numer_far * weight_far[..., None]) / combined[
        ..., None
    ]
    return (output, highest + jnp.log(combined))


def project(left_side, right_side):
    return jnp.dot(left_side, right_side, preferred_element_type=jnp.float32)


def per_device(tile_embed, tile_source, slide_len, grad_out, w_query, w_key, w_value, w_out):
    owned_rows = tile_embed[0]
    source = tile_source[0]
    row_count, features = owned_rows.shape
    stripes = lax.axis_size("seq")
    stripe = lax.axis_index("seq")
    portion = row_count // stripes
    owner_dev = source // row_count
    ordering = jnp.argsort(owner_dev, stable=True)
    wanted = (source % row_count)[ordering].reshape(stripes, portion)
    requested = lax.all_to_all(wanted, "seq", split_axis=0, concat_axis=0, tiled=True)
    picked = jnp.take(owned_rows, requested.reshape(-1), axis=0).reshape(stripes, portion, features)
    arrived = lax.all_to_all(picked, "seq", split_axis=0, concat_axis=0, tiled=True).reshape(
        row_count, features
    )
    embedded = jnp.zeros_like(arrived).at[ordering].set(arrived)
    length = slide_len[0]
    upstream_in = grad_out[0]
    head_dim = features // HEADS
    scaling = head_dim ** (-0.5)
    positions = stripe * row_count + jnp.arange(row_count)
    valid_rows = positions < length
    queries = project(embedded, w_query).astype(jnp.bfloat16).reshape(row_count, HEADS, head_dim)
    key_rows = project(embedded, w_key).astype(jnp.bfloat16).reshape(row_count, HEADS, head_dim)
    values = project(embedded, w_value).astype(jnp.bfloat16).reshape(row_count, HEADS, head_dim)
    local_ok = jnp.broadcast_to(valid_rows[:, None], (row_count, HEADS))
    local_part = heads_map(
        head_forward, (queries, key_rows, values, local_ok), row_count // SEG, scaling
    )
    sparse_q = sparse_rows(queries, RATE).astype(jnp.bfloat16)
    sparse_k = sparse_rows(key_rows, RATE).astype(jnp.bfloat16)
    sparse_v = sparse_rows(values, RATE).astype(jnp.bfloat16)
    near_count = sparse_k.shape[0]
    far_k, far_v = sent_together(
        (sparse_k.reshape(near_count, features), sparse_v.reshape(near_count, features)),
        "seq",
        0,
        1,
    )
    far_count = far_k.shape[0]
    far_k = far_k.reshape(far_count, HEADS, head_dim)
    far_v = far_v.reshape(far_count, HEADS, head_dim)
    sparse_pos = jnp.arange(far_count)[:, None] * RATE + (jnp.arange(HEADS) % RATE)[None, :]
    sparse_ok = sparse_pos < length
    remote = heads_map(head_forward, (sparse_q, far_k, far_v, sparse_ok), 1, scaling)
    output, log_total = merge_parts(local_part, remote, RATE)
    attended = (
        (output * valid_rows[:, None, None]).astype(jnp.bfloat16).reshape(row_count, features)
    )
    encoded = (embedded.astype(jnp.float32) + project(attended, w_out)).astype(jnp.bfloat16)
    upstream = (
        (project(upstream_in, w_out.T) * valid_rows[:, None])
        .astype(jnp.bfloat16)
        .reshape(row_count, HEADS, head_dim)
    )
    deltas = jnp.sum(upstream.astype(jnp.float32) * output, axis=-1)
    grad_outproj = jnp.einsum(
        "td,te->de", attended, upstream_in, preferred_element_type=jnp.float32
    )
    local_grads = heads_map(
        head_backward,
        (queries, key_rows, values, local_ok, log_total, upstream, deltas),
        row_count // SEG,
        scaling,
    )
    sparse_up = sparse_rows(upstream, RATE).astype(jnp.bfloat16)
    sparse_delta = sparse_rows(deltas[..., None], RATE)[..., 0]
    sparse_total = sparse_rows(log_total[..., None], RATE)[..., 0]
    remote_grads = heads_map(
        head_backward,
        (sparse_q, far_k, far_v, sparse_ok, sparse_total, sparse_up, sparse_delta),
        1,
        scaling,
    )
    key_back, value_back = side_by_side(
        (
            remote_grads[1].reshape(far_count, features),
            remote_grads[2].reshape(far_count, features),
        ),
        "seq",
        0,
        1,
    )
    key_back = key_back.reshape(near_count, HEADS, head_dim)
    value_back = value_back.reshape(near_count, HEADS, head_dim)
    query_far = remote_grads[0]
    query_grad = (
        (local_grads[0] + spread_rows(query_far, RATE, 0.0))
        .astype(jnp.bfloat16)
        .reshape(row_count, features)
    )
    key_grad = (
        (local_grads[1] + spread_rows(key_back, RATE, 0.0))
        .astype(jnp.bfloat16)
        .reshape(row_count, features)
    )
    value_grad = (
        (local_grads[2] + spread_rows(value_back, RATE, 0.0))
        .astype(jnp.bfloat16)
        .reshape(row_count, features)
    )
    embed_grad = upstream_in.astype(jnp.float32) + project(query_grad, w_query.T)
    embed_grad = embed_grad + project(key_grad, w_key.T)
    embed_grad = (embed_grad + project(value_grad, w_value.T)).astype(jnp.bfloat16)
    grad_query = jnp.einsum("td,te->de", embedded, query_grad, preferred_element_type=jnp.float32)
    grad_key = jnp.einsum("td,te->de", embedded, key_grad, preferred_element_type=jnp.float32)
    grad_value = jnp.einsum("td,te->de", embedded, value_grad, preferred_element_type=jnp.float32)
    summed = lax.psum((grad_query, grad_key, grad_value, grad_outproj), ("seq", "rep"))
    return (encoded[None], embed_grad[None], summed[0], summed[1], summed[2], summed[3])


def solution(mesh):
    return jax.shard_map(
        per_device,
        mesh=mesh,
        in_specs=(
            P("rep", "seq", None),
            P("rep", "seq"),
            P("rep"),
            P("rep", "seq", None),
            P(),
            P(),
            P(),
            P(),
        ),
        out_specs=(P("rep", "seq", None), P("rep", "seq", None), P(), P(), P(), P()),
        check_vma=False,
    )
```

profile of v0, /device:TPU:1, one launch (start us, length us, event | category | flops | bytes accessed | tf_op | source)
XLA Modules:
  0.0 927.7 jit_solution(13894790200978015584)
XLA Ops:
  8.0 4.4 sort.17
  12.4 4.5 gather_fusion
  16.9 13.8 %all_to_all.14 = s32[8,1,128]{2,1,0:T(1,128)S(1)} all-to-all(s32[8,1,128]{2,1,0:T(1,128)S(1)} %bitcast.386), channel_id=1, replica_groups=mesh['seq'=8,'rep'=16] {'seq'}, dimensions={0} | all-to-all | bytes 8192 | tf_op jit(solution)/shard_map/all_to_all | solution.py:135
  30.7 4.0 gather_fusion.1
  36.1 4.4 all-to-all-start.1
  47.3 4.8 copy.100
  55.3 7.8 reshape.434
  65.1 6.4 scatter_custom_fusion
  76.8 7.8 reshape.431
  90.0 7.8 reshape.432
  97.8 4.3 convolution_convert_fusion
  105.1 7.8 reshape.433
  112.9 14.1 %select_reduce_fusion = (bf16[64,16,48]{2,1,0:T(8,128)(2,1)S(1)}, bf16[64,16,48]{2,1,0:T(8,128)(2,1)}, bf16[64,16,48]{2,1,0:T(8,128)(2,1)}, bf16[64,16,48]{2,1,0:T(8,128)(2,1)}) fusion(f32[64,16,16,48]{3,2,1,0:T(8,128)} %reshape.434, pred[16,16]{1,0:T(8,128)(4,1)} %copy-done.23, f32[64,16,16,48]{3,2,1,0:T(8,128)} %reshape.432, ...), kind=kLoop, calls=%fused_computation.133 | loop fusion | flops 6094848 | bytes 12976384 | tf_op jit(solution)/shard_map/reduce_sum | solution.py:38
  144.3 142.6 %while.56 = (s32[]{:T(128)}, f32[16,1024,48]{1,2,0:T(8,128)}, f32[16,1024]{1,0:T(8,128)S(1)}, f32[16,1024]{1,0:T(8,128)S(1)}, pred[16,1024]{1,0:T(8,128)(4,1)S(1...) while((s32[]{:T(128)}, f32[16,1024,48]{1,2,0:T(8,128)}, ...), condition=%wide.region_5.6_spmd, body=%wide.region_2.5_spmd.sunk | while | flops 212858880 | bytes 30383244 | solution.py:102
  158.0 4.0 fusion.204
  166.9 4.2 fusion.204
  176.0 4.0 fusion.204
  184.9 4.0 fusion.204
  193.8 4.0 fusion.204
  202.7 4.0 fusion.204
  211.6 4.0 fusion.204
  220.5 4.0 fusion.204
  229.5 4.0 fusion.204
  238.4 4.0 fusion.204
  247.2 4.0 fusion.204
  256.1 4.0 fusion.204
  265.0 4.0 fusion.204
  273.9 4.0 fusion.204
  282.8 4.0 fusion.204
  287.0 7.9 copy.83
  301.3 42.2 %while.57 = (s32[]{:T(128)}, f32[16,64,48]{1,2,0:T(8,128)S(1)}, f32[16,64]{1,0:T(8,128)S(1)}, f32[16,64]{1,0:T(8,128)S(1)}, pred[16,512]{1,0:T(8,128)(4,1)S(1)},...) while((s32[]{:T(128)}, f32[16,64,48]{1,2,0:T(8,128)S(1)}, ...), condition=%wide.region_12.13_spmd, body=%wide.region_9.12_spmd.sunk | while | flops 6520706 | bytes 702321 | solution.py:102
  346.2 13.4 %multiply_convert_fusion.1 = (bf16[1024,16,48]{2,1,0:T(8,128)(2,1)}, f32[1024,16,48]{2,1,0:T(8,128)S(1)}) fusion(f32[1024]{0:T(1024)S(1)} %copy-done.25, f32[1024,16]{1,0:T(8,128)} %copy.97, f32[1024,16]{1,0:T(8,128)S(1)} %copy.96, f32[64,16,48]{2,1,0:T(8,128)S(1)} %copy.95, pred[1024,16]{1,0:T(8,128)(4,1)S(1)} %copy.94, f32[1024,16]{1,0:T(8,128)S(1)} %copy.93, ...), kind=kLoop, calls=%fused_computation.135 | loop fusion | flops 5505024 | bytes 8278016 | tf_op jit(solution)/shard_map/convert_element_type | solution.py:172
  362.9 103.9 %while.59 = (s32[]{:T(128)}, f32[16,64,48]{1,2,0:T(8,128)S(1)}, f32[16,512,48]{1,2,0:T(8,128)}, f32[16,512,48]{1,2,0:T(8,128)}, pred[16,512]{1,0:T(8,128)(4,1)S(...) while((s32[]{:T(128)}, f32[16,64,48]{1,2,0:T(8,128)S(1)}, ...), condition=%wide.region_20.21_spmd, body=%wide.region_19.20_spmd.sunk | while | flops 15985666 | bytes 1278077 | solution.py:102
  481.0 181.1 %while.58 = (s32[]{:T(128)}, f32[16,1024,48]{1,2,0:T(8,128)}, f32[16,1024,48]{1,2,0:T(8,128)}, f32[16,1024,48]{1,2,0:T(8,128)}, pred[16,1024]{1,0:T(8,128)(4,1)S...) while((s32[]{:T(128)}, f32[16,1024,48]{1,2,0:T(8,128)}, ...), condition=%wide.region_15.16_spmd, body=%wide.region_14.15_spmd.sunk | while | flops 513900544 | bytes 21337212 | solution.py:102
  662.5 7.9 copy.102
  670.3 7.8 copy.112
  678.2 7.8 copy.115
  686.0 5.5 copy.98
  691.5 4.2 fusion.114
  699.3 15.1 %fusion.110 = (bf16[1024,16,48]{2,1,0:T(8,128)(2,1)}, bf16[1024,16,48]{2,1,0:T(8,128)(2,1)}, bf16[1024,16,48]{2,1,0:T(8,128)(2,1)}) fusion(f32[16,1024,48]{2,0,1:T(8,128)} %copy.102, f32[64,16,48]{2,1,0:T(8,128)S(1)} %copy.110, pred[1024,16]{1,0:T(8,128)(4,1)} %copy-done.14, f32[64,16,48]{2,1,0:T(8,128)S(1)} %copy.113, f32[16,1024,48]{2,0,1:T(8,128)} %copy.112, ...), kind=kLoop, calls=%fused_computation.127 | loop fusion | flops 7077888 | bytes 14761984 | tf_op jit(solution)/shard_map/convert_element_type | solution.py:213
  714.4 5.5 copy.111
  719.9 4.2 fusion.132
  724.2 5.5 copy.114
  729.7 4.2 fusion.133
  734.0 4.4 copy.117
  738.4 4.2 fusion.134
  742.7 5.0 fusion.117
  753.6 157.5 %all-reduce.3.cloned.1.call-done = (f32[768,768]{1,0:T(8,128)}, f32[768,768]{1,0:T(8,128)}, f32[768,768]{1,0:T(8,128)}, f32[768,768]{1,0:T(8,128)}) async-done(((f32[768,768]{1,0:T(8,128)}, f32[768,768]{1,0:T(8,128)}, f32[768,768]{1,0:T(8,128)}, f32[768,768]{1,0:T(8,128)}), (f32[768,768]{1,0:T(8,128)}, f32[768,768]{1,0:T(8,128)}, f32[768,768]{1,0:T(8,128)}, ...) | async-done | bytes 9437200 | tf_op jit(solution)/shard_map/psum | solution.py:232
  (581 shorter events, 497.7 us)
Async XLA Ops:
  7.2 23.6 %copy-start = (bf16[1,1024,768]{2,1,0:T(8,128)(2,1)S(1)}, bf16[1,1024,768]{2,1,0:T(8,128)(2,1)}, u32[]{:S(2)}) copy-start(bf16[1,1024,768]{2,1,0:T(8,128)(2,1)} %param.16) | copy-start | bytes 4718596
  36.1 6.4 copy-start.8
  36.1 29.0 %all-to-all-start.1 = ((bf16[8,128,768]{2,1,0:T(8,128)(2,1)}), bf16[8,128,768]{2,1,0:T(8,128)(2,1)}, u32[]{:S(2)}, u32[]{:S(2)}) async-start(bf16[8,128,768]{2,1,0:T(8,128)(2,1)} %broadcast_select_fusion), calls=%async_computation.1 | async-start | bytes 3145728 | tf_op jit(solution)/shard_map/all_to_all | solution.py:137
  40.5 255.1 %all-gather.2.cloned.1.call-start = ((), (), s32[]{:S(2)}) async-start(), calls=%async_computation.3 | async-start | bytes 1769472 | tf_op jit(solution)/shard_map/all_gather | solution.py:14
  63.7 1.4 copy-start.21
  64.4 281.8 %copy-start.14 = (pred[1024,16]{1,0:T(8,128)(4,1)}, pred[1024,16]{1,0:T(8,128)(4,1)S(1)}, u32[]{:S(2)}) copy-start(pred[1024,16]{1,0:T(8,128)(4,1)S(1)} %copy.94) | copy-start | bytes 49156
  71.5 3.3 copy-start.10
  132.4 563.3 %reduce-scatter.4.cloned.1.call-start = ((), (), s32[]{:S(2)}) async-start(), calls=%async_computation.4 | async-start | bytes 3538944
  135.9 3.2 copy-start.4
  139.0 3.2 copy-start.28
  139.0 5.3 copy-start.19
  139.0 5.3 copy-start.20
  144.3 142.7 %copy-start.16 = (bf16[64,16,48]{2,1,0:T(8,128)(2,1)S(1)}, bf16[64,16,48]{2,1,0:T(8,128)(2,1)}, u32[]{:S(2)}) copy-start(bf16[64,16,48]{2,1,0:T(8,128)(2,1)} %get-tuple-element.310) | copy-start | bytes 294916
  146.1 1.9 copy-start.2
  155.0 1.9 copy-start.2
  163.9 1.9 copy-start.2
  173.0 1.9 copy-start.2
  182.0 1.9 copy-start.2
  190.9 1.9 copy-start.2
  199.8 1.9 copy-start.2
  208.6 1.9 copy-start.2
  217.6 1.9 copy-start.2
  226.5 1.9 copy-start.2
  235.4 1.9 copy-start.2
  244.3 1.9 copy-start.2
  253.2 1.9 copy-start.2
  262.1 1.9 copy-start.2
  271.0 1.9 copy-start.2
  279.8 1.9 copy-start.2
  299.2 2.1 copy-start.18
  299.2 2.1 copy-start.26
  299.2 2.1 copy-start.27
  343.4 2.4 copy-start.17
  343.4 2.7 copy-start.25
  346.2 13.4 %copy-start.3 = (bf16[1024,16,48]{2,1,0:T(8,128)(2,1)S(1)}, bf16[1024,16,48]{2,1,0:T(8,128)(2,1)}, u32[]{:S(2)}) copy-start(bf16[1024,16,48]{2,1,0:T(8,128)(2,1)} %copy.100) | copy-start | bytes 4718596
  359.6 3.0 copy-start.22
  474.7 436.5 %all-reduce.3.cloned.1.call-start = ((), (), s32[]{:S(2)}) async-start(), calls=%async_computation.5 | async-start | bytes 18874368 | tf_op jit(solution)/shard_map/psum | solution.py:232
  686.0 5.5 copy-start.9
  714.4 5.5 copy-start.11
  742.7 5.0 copy-start.12
  742.7 5.0 copy-start.29
  747.7 1.5 copy-start.13
  747.7 1.7 copy-start.30
  749.4 1.5 copy-start.15
  911.1 3.4 copy-start.7
  914.5 2.5 copy-start.6
  917.0 2.5 copy-start.5
  917.0 3.9 copy-start.1
  (2 other events, 1.1 us)
Sparse Core Ops, SparseCore 0:
  132.6 52.8 all-gather.1
  474.8 81.6 reduce-scatter.3
  742.8 168.2 all-reduce.2
where the time goes:
time: 942 us; the launch traced here: 928 us
  matrix products  454 us (48%)
  local copies, waits for them, and re-layouts  204 us (22%)
  waiting for transfers between devices  158 us (17%)
  other arithmetic  76.5 us (8%)
  between operations  15.1 us (2%)
  blocking collectives  13.8 us (1%)
    dot_general x224, matrix products, product(): jnp.einsum(pattern, left_side, right_side, preferred_element_type=jnp.flo...  413 us
    psum x1, waiting for transfers between devices, per_device(): lax.psum((grad_query, grad_key, grad_value, grad_outproj), ('seq', 'rep'))  158 us
    while x9, local copies, waits for them, and re-layouts, heads_map(): lax.map(lambda members: function(*members, pieces, scaling), transposed)  35.9 us
    while x32, local copies, waits for them, and re-layouts  30.8 us
    convert_element_type x6, local copies, waits for them, and re-layouts, sparse_rows(): dense.astype(jnp.float32)  30.7 us
    dot_general x8, matrix products, project(): return jnp.dot(left_side, right_side, preferred_element_type=jnp.float32)  24 us
  transfers between devices with their start and end apart: 4, of which 1 were waited for; matrix products, arithmetic and copies ran while one was open for 41% of the time, Pallas kernels for 0%

commit v1 on v0

--- a/solution.py
+++ b/solution.py
@@ -229,7 +229,7 @@
     grad_query = jnp.einsum("td,te->de", embedded, query_grad, preferred_element_type=jnp.float32)
     grad_key = jnp.einsum("td,te->de", embedded, key_grad, preferred_element_type=jnp.float32)
     grad_value = jnp.einsum("td,te->de", embedded, value_grad, preferred_element_type=jnp.float32)
-    summed = lax.psum((grad_query, grad_key, grad_value, grad_outproj), ("seq", "rep"))
+    summed = lax.psum(lax.psum((grad_query, grad_key, grad_value, grad_outproj), "rep"), "seq")
     return (encoded[None], embed_grad[None], summed[0], summed[1], summed[2], summed[3])
 
 

time: 942 us -> 1310 us (1.39)
  waiting for transfers between devices: 158 us -> 526 us
    psum x1 -> x2, waiting for transfers between devices: 158 us -> 526 us  [the longest x1 377 us: per_device(): lax.psum(lax.psum((grad_query, grad_key, grad_value, grad_outproj), 'rep'...]
  transfers between devices with their start and end apart: 4 -> 5, of which waited for: 1 -> 2; matrix products, arithmetic and copies ran while one was open for 41% -> 30% of each run, Pallas kernels for 0% -> 0%
where the time goes in v1:
time: 1310 us; the launch traced here: 1300 us
  waiting for transfers between devices  526 us (40%)
  matrix products  453 us (35%)
  local copies, waits for them, and re-layouts  204 us (16%)
  other arithmetic  76.5 us (6%)
  between operations  15.1 us (1%)
  blocking collectives  13.8 us (1%)
    dot_general x224, matrix products, product(): jnp.einsum(pattern, left_side, right_side, preferred_element_type=jnp.flo...  413 us
    psum x1, waiting for transfers between devices, per_device(): lax.psum(lax.psum((grad_query, grad_key, grad_value, grad_outproj), 'rep'...  377 us
    psum x1, waiting for transfers between devices, per_device(): lax.psum((grad_query, grad_key, grad_value, grad_outproj), 'rep')  149 us
    while x9, local copies, waits for them, and re-layouts, heads_map(): lax.map(lambda members: function(*members, pieces, scaling), transposed)  35.9 us
    while x32, local copies, waits for them, and re-layouts  31 us
    convert_element_type x6, local copies, waits for them, and re-layouts, sparse_rows(): dense.astype(jnp.float32)  30.7 us
  transfers between devices with their start and end apart: 5, of which 2 were waited for; matrix products, arithmetic and copies ran while one was open for 30% of the time, Pallas kernels for 0%

profile of v1, /device:TPU:1, one launch (start us, length us, event | category | flops | bytes accessed | tf_op | source)
XLA Modules:
  0.0 1295.9 jit_solution(10087760105281292511)
XLA Ops:
  8.0 4.4 sort.17
  12.4 4.5 gather_fusion
  16.9 13.8 %all_to_all.14 = s32[8,1,128]{2,1,0:T(1,128)S(1)} all-to-all(s32[8,1,128]{2,1,0:T(1,128)S(1)} %bitcast.386), channel_id=1, replica_groups=mesh['seq'=8,'rep'=16] {'seq'}, dimensions={0} | all-to-all | bytes 8192 | tf_op jit(solution)/shard_map/all_to_all | solution.py:135
  30.7 4.0 gather_fusion.1
  36.1 4.4 all-to-all-start.1
  47.3 4.8 copy.100
  55.2 7.8 reshape.434
  65.1 6.4 scatter_custom_fusion
  76.8 7.8 reshape.431
  90.0 7.8 reshape.432
  97.8 4.3 convolution_convert_fusion
  105.2 7.8 reshape.433
  113.0 14.1 %select_reduce_fusion = (bf16[64,16,48]{2,1,0:T(8,128)(2,1)S(1)}, bf16[64,16,48]{2,1,0:T(8,128)(2,1)}, bf16[64,16,48]{2,1,0:T(8,128)(2,1)}, bf16[64,16,48]{2,1,0:T(8,128)(2,1)}) fusion(f32[64,16,16,48]{3,2,1,0:T(8,128)} %reshape.434, pred[16,16]{1,0:T(8,128)(4,1)} %copy-done.23, f32[64,16,16,48]{3,2,1,0:T(8,128)} %reshape.432, ...), kind=kLoop, calls=%fused_computation.133 | loop fusion | flops 6094848 | bytes 12976384 | tf_op jit(solution)/shard_map/reduce_sum | solution.py:38
  144.3 142.8 %while.56 = (s32[]{:T(128)}, f32[16,1024,48]{1,2,0:T(8,128)}, f32[16,1024]{1,0:T(8,128)S(1)}, f32[16,1024]{1,0:T(8,128)S(1)}, pred[16,1024]{1,0:T(8,128)(4,1)S(1...) while((s32[]{:T(128)}, f32[16,1024,48]{1,2,0:T(8,128)}, ...), condition=%wide.region_5.6_spmd, body=%wide.region_2.5_spmd.sunk | while | flops 212858880 | bytes 30383244 | solution.py:102
  158.0 4.0 fusion.204
  166.9 4.2 fusion.204
  176.1 4.0 fusion.204
  185.0 4.0 fusion.204
  193.9 4.0 fusion.204
  202.8 4.0 fusion.204
  211.7 4.0 fusion.204
  220.6 4.0 fusion.204
  229.5 4.0 fusion.204
  238.4 4.0 fusion.204
  247.4 4.0 fusion.204
  256.3 4.0 fusion.204
  265.2 4.0 fusion.204
  283.0 4.0 fusion.204
  287.2 7.9 copy.83
  301.4 42.2 %while.57 = (s32[]{:T(128)}, f32[16,64,48]{1,2,0:T(8,128)S(1)}, f32[16,64]{1,0:T(8,128)S(1)}, f32[16,64]{1,0:T(8,128)S(1)}, pred[16,512]{1,0:T(8,128)(4,1)S(1)},...) while((s32[]{:T(128)}, f32[16,64,48]{1,2,0:T(8,128)S(1)}, ...), condition=%wide.region_12.13_spmd, body=%wide.region_9.12_spmd.sunk | while | flops 6520706 | bytes 702321 | solution.py:102
  346.3 13.4 %multiply_convert_fusion.1 = (bf16[1024,16,48]{2,1,0:T(8,128)(2,1)}, f32[1024,16,48]{2,1,0:T(8,128)S(1)}) fusion(f32[1024]{0:T(1024)S(1)} %copy-done.25, f32[1024,16]{1,0:T(8,128)} %copy.97, f32[1024,16]{1,0:T(8,128)S(1)} %copy.96, f32[64,16,48]{2,1,0:T(8,128)S(1)} %copy.95, pred[1024,16]{1,0:T(8,128)(4,1)S(1)} %copy.94, f32[1024,16]{1,0:T(8,128)S(1)} %copy.93, ...), kind=kLoop, calls=%fused_computation.135 | loop fusion | flops 5505024 | bytes 8278016 | tf_op jit(solution)/shard_map/convert_element_type | solution.py:172
  363.1 103.9 %while.59 = (s32[]{:T(128)}, f32[16,64,48]{1,2,0:T(8,128)S(1)}, f32[16,512,48]{1,2,0:T(8,128)}, f32[16,512,48]{1,2,0:T(8,128)}, pred[16,512]{1,0:T(8,128)(4,1)S(...) while((s32[]{:T(128)}, f32[16,64,48]{1,2,0:T(8,128)S(1)}, ...), condition=%wide.region_20.21_spmd, body=%wide.region_19.20_spmd.sunk | while | flops 15985666 | bytes 1278077 | solution.py:102
  481.1 181.1 %while.58 = (s32[]{:T(128)}, f32[16,1024,48]{1,2,0:T(8,128)}, f32[16,1024,48]{1,2,0:T(8,128)}, f32[16,1024,48]{1,2,0:T(8,128)}, pred[16,1024]{1,0:T(8,128)(4,1)S...) while((s32[]{:T(128)}, f32[16,1024,48]{1,2,0:T(8,128)}, ...), condition=%wide.region_15.16_spmd, body=%wide.region_14.15_spmd.sunk | while | flops 513900544 | bytes 21337212 | solution.py:102
  662.5 7.9 copy.102
  670.4 7.8 copy.112
  678.2 7.9 copy.115
  686.1 5.5 copy.98
  691.6 4.2 fusion.114
  699.3 15.1 %fusion.110 = (bf16[1024,16,48]{2,1,0:T(8,128)(2,1)}, bf16[1024,16,48]{2,1,0:T(8,128)(2,1)}, bf16[1024,16,48]{2,1,0:T(8,128)(2,1)}) fusion(f32[16,1024,48]{2,0,1:T(8,128)} %copy.102, f32[64,16,48]{2,1,0:T(8,128)S(1)} %copy.110, pred[1024,16]{1,0:T(8,128)(4,1)} %copy-done.14, f32[64,16,48]{2,1,0:T(8,128)S(1)} %copy.113, f32[16,1024,48]{2,0,1:T(8,128)} %copy.112, ...), kind=kLoop, calls=%fused_computation.127 | loop fusion | flops 7077888 | bytes 14761984 | tf_op jit(solution)/shard_map/convert_element_type | solution.py:213
  714.5 5.5 copy.111
  720.0 4.2 fusion.132
  724.2 5.5 copy.114
  729.7 4.2 fusion.133
  734.0 4.4 copy.117
  738.4 4.2 fusion.134
  742.8 149.1 %all-reduce.5.cloned.1.call-done = (f32[768,768]{1,0:T(8,128)}, f32[768,768]{1,0:T(8,128)}, f32[768,768]{1,0:T(8,128)}, f32[768,768]{1,0:T(8,128)}) async-done(((f32[768,768]{1,0:T(8,128)}, f32[768,768]{1,0:T(8,128)}, f32[768,768]{1,0:T(8,128)}, f32[768,768]{1,0:T(8,128)}), (f32[768,768]{1,0:T(8,128)}, f32[768,768]{1,0:T(8,128)}, f32[768,768]{1,0:T(8,128)}, ...) | async-done | bytes 9437200 | tf_op jit(solution)/shard_map/psum | solution.py:232
  891.9 5.0 fusion.117
  902.7 376.6 %all-reduce.7.cloned.1.call-done = (f32[768,768]{1,0:T(8,128)}, f32[768,768]{1,0:T(8,128)}, f32[768,768]{1,0:T(8,128)}, f32[768,768]{1,0:T(8,128)}) async-done(((f32[768,768]{1,0:T(8,128)}, f32[768,768]{1,0:T(8,128)}, f32[768,768]{1,0:T(8,128)}, f32[768,768]{1,0:T(8,128)}), (f32[768,768]{1,0:T(8,128)}, f32[768,768]{1,0:T(8,128)}, f32[768,768]{1,0:T(8,128)}, ...) | async-done | bytes 9437200 | tf_op jit(solution)/shard_map/psum | solution.py:232
  (584 shorter events, 501.8 us)
Async XLA Ops:
  7.2 23.6 %copy-start = (bf16[1,1024,768]{2,1,0:T(8,128)(2,1)S(1)}, bf16[1,1024,768]{2,1,0:T(8,128)(2,1)}, u32[]{:S(2)}) copy-start(bf16[1,1024,768]{2,1,0:T(8,128)(2,1)} %param.16) | copy-start | bytes 4718596
  36.1 6.4 copy-start.8
  36.1 29.0 %all-to-all-start.1 = ((bf16[8,128,768]{2,1,0:T(8,128)(2,1)}), bf16[8,128,768]{2,1,0:T(8,128)(2,1)}, u32[]{:S(2)}, u32[]{:S(2)}) async-start(bf16[8,128,768]{2,1,0:T(8,128)(2,1)} %broadcast_select_fusion), calls=%async_computation.1 | async-start | bytes 3145728 | tf_op jit(solution)/shard_map/all_to_all | solution.py:137
  40.5 255.2 %all-gather.2.cloned.1.call-start = ((), (), s32[]{:S(2)}) async-start(), calls=%async_computation.3 | async-start | bytes 1769472 | tf_op jit(solution)/shard_map/all_gather | solution.py:14
  64.4 281.9 %copy-start.14 = (pred[1024,16]{1,0:T(8,128)(4,1)}, pred[1024,16]{1,0:T(8,128)(4,1)S(1)}, u32[]{:S(2)}) copy-start(pred[1024,16]{1,0:T(8,128)(4,1)S(1)} %copy.94) | copy-start | bytes 49156
  71.5 3.3 copy-start.10
  132.4 563.3 %reduce-scatter.4.cloned.1.call-start = ((), (), s32[]{:S(2)}) async-start(), calls=%async_computation.4 | async-start | bytes 3538944
  135.9 3.2 copy-start.4
  139.0 3.2 copy-start.28
  139.0 5.2 copy-start.19
  139.0 5.2 copy-start.20
  144.3 142.8 %copy-start.16 = (bf16[64,16,48]{2,1,0:T(8,128)(2,1)S(1)}, bf16[64,16,48]{2,1,0:T(8,128)(2,1)}, u32[]{:S(2)}) copy-start(bf16[64,16,48]{2,1,0:T(8,128)(2,1)} %get-tuple-element.310) | copy-start | bytes 294916
  146.1 1.9 copy-start.2
  155.0 1.9 copy-start.2
  163.9 1.9 copy-start.2
  173.1 1.9 copy-start.2
  182.0 1.9 copy-start.2
  190.9 1.9 copy-start.2
  199.8 1.9 copy-start.2
  208.7 1.9 copy-start.2
  217.6 1.9 copy-start.2
  226.6 1.9 copy-start.2
  235.5 1.9 copy-start.2
  244.4 1.9 copy-start.2
  253.3 1.9 copy-start.2
  262.2 1.9 copy-start.2
  271.1 1.9 copy-start.2
  280.0 1.9 copy-start.2
  299.3 2.1 copy-start.18
  299.3 2.1 copy-start.26
  299.3 2.1 copy-start.27
  343.6 2.4 copy-start.17
  343.6 2.7 copy-start.25
  346.3 13.4 %copy-start.3 = (bf16[1024,16,48]{2,1,0:T(8,128)(2,1)S(1)}, bf16[1024,16,48]{2,1,0:T(8,128)(2,1)}, u32[]{:S(2)}) copy-start(bf16[1024,16,48]{2,1,0:T(8,128)(2,1)} %copy.100) | copy-start | bytes 4718596
  359.7 3.0 copy-start.22
  474.8 417.1 %all-reduce.5.cloned.1.call-start = ((), (), s32[]{:S(2)}) async-start(), calls=%async_computation.5 | async-start | bytes 18874368 | tf_op jit(solution)/shard_map/psum | solution.py:232
  686.1 5.5 copy-start.9
  714.5 5.5 copy-start.11
  742.7 536.6 %all-reduce.7.cloned.1.call-start = ((), (), s32[]{:S(2)}) async-start(), calls=%async_computation.6 | async-start | bytes 18874368 | tf_op jit(solution)/shard_map/psum | solution.py:232
  891.9 5.0 copy-start.12
  891.9 5.0 copy-start.29
  896.8 1.5 copy-start.13
  896.8 1.7 copy-start.30
  898.6 1.5 copy-start.15
  1279.3 3.4 copy-start.7
  1282.7 2.5 copy-start.6
  1285.2 2.5 copy-start.5
  1285.2 3.9 copy-start.1
  (3 other events, 2.5 us)
Sparse Core Ops, SparseCore 0:
  132.6 52.8 all-gather.1
  474.9 81.6 reduce-scatter.3
  742.8 148.9 all-reduce.4
  894.4 384.8 all-reduce.6
